TPU v7x, 512 devices: a whole 4x4x16 slice. The times are simulated.
512 devices in a mesh: feeder: 32 (over x, y, core), scen: 16 (over z).
Axes of the slice: x: 4, y: 4, z: 16, core: 2. Of those that a mesh axis runs over, the one named last changes fastest.
Arguments:
- anchor: bfloat16 [256, 24, 16384], P('scen', None, 'feeder'), may hold values from -6 to 6
- cost_lin: bfloat16 [256, 24, 16384], P('scen', None, 'feeder'), may hold values from -6 to 6
- dual: float32 [256, 24, 16384], P('scen', None, 'feeder'), may hold values from -4 to 4
- target: float32 [256, 24], P('scen'), may hold values from -4 to 4
- leaf_weight: float32 [256], P('scen'), may hold values from 1 to 10
- q_mat: bfloat16 [16384, 512], P('feeder'), may hold values from -0.25 to 0.25
- diag_gain: float32 [16384], P('feeder'), may hold values from 0.5 to 2
- block_mask: int32 [32, 4, 4], P('feeder'), may hold values from 0 to 1, as said below
- ancestor: int32 [24, 256], P(None, 'scen'), may hold values from 0 to 255, as said below
Outputs:
- setpoints: float32 [256, 24, 16384], P('scen', None, 'feeder')
- average: float32 [256, 24, 16384], P('scen', None, 'feeder')
- new_dual: float32 [256, 24, 16384], P('scen', None, 'feeder')
Inputs may be any that keep to these rules, and one draw needn't show every extreme that they name: `block_mask`: every diagonal block is present; the share of present off-diagonal blocks differs from feeder to feeder. ancestor[t, s] is the first leaf of the section-t tree node that holds leaf s: the leaves of a node are consecutive, ancestor[0, s] = 0, and every section-t node lies inside one section-(t-1) node. Nodes may span several groups at any section.
All inputs are finite; a program needn't handle non-finite values.
Results may differ from a plain program's by a relative error of at most 0.0003.
Values sent between devices are 32-bit elements; how exact they have to be, the bound alone decides.
No kernel may reach another device: no remote copies, remote signals or barrier semaphores. Data moves between devices by JAX's collectives and lax.ppermute only.
A program may use at most 64 MiB of HBM per device.

v0:
```python
import jax
import jax.numpy as jnp
from jax import lax
from jax.sharding import PartitionSpec as P

PROX_ITERS = 8
penalty = 1.0
step_size = 0.08
coupling = 4.0
power_limit = 2.0


def link_terms(earlier, later):
    return (
        later[0] + later[2][:, None] * earlier[0],
        later[1] + later[2] * earlier[1],
        earlier[2] * later[2],
    )


def local(anchor, cost_lin, dual, target, leaf_weight, q_mat, diag_gain, block_mask, ancestor):
    leaves, sections, nodes = anchor.shape
    rows = leaves * sections
    count = block_mask.shape[1]
    width = nodes // count
    total_nodes = lax.axis_size("feeder") * nodes
    start_pt = anchor.astype(jnp.float32)
    fixed_part = cost_lin.astype(jnp.float32) + dual - penalty * start_pt
    diag_term = 2.0 * diag_gain + penalty
    expand = jnp.repeat(jnp.repeat(block_mask[0], width, axis=0), width, axis=1).astype(
        jnp.bfloat16
    )
    q_eff = q_mat * expand
    state = start_pt
    for sweep in range(PROX_ITERS):
        flat = state.reshape(rows, nodes).astype(jnp.bfloat16)
        image = jnp.dot(flat, q_eff, preferred_element_type=jnp.float32)
        head = lax.psum(jnp.sum(state, axis=2), "feeder") / total_nodes
        grad = image.reshape(leaves, sections, nodes) + diag_term * state + fixed_part
        grad = grad + coupling * (head - target)[:, :, None]
        state = jnp.clip(state - step_size * grad, -power_limit, power_limit)
    highest = lax.Precision.HIGHEST
    weighted = leaf_weight[:, None, None] * state
    first_leaf = lax.axis_index("scen") * leaves
    local_id = jnp.maximum(ancestor - first_leaf, 0)
    slot_ids = jnp.arange(leaves, dtype=jnp.int32)
    member = (local_id[:, None, :] == slot_ids[None, :, None]).astype(jnp.float32)
    seg_sums = jnp.einsum("tgl,ltn->tgn", member, weighted, precision=highest)
    seg_weights = jnp.einsum("tgl,l->tg", member, leaf_weight, precision=highest)
    last_pick = (slot_ids[None, :] == local_id[:, leaves - 1][:, None]).astype(jnp.float32)
    first_pick = (slot_ids[None, :] == 0).astype(jnp.float32)
    tail_sum = jnp.einsum("tg,tgn->tn", last_pick, seg_sums, precision=highest)
    tail_weight = jnp.sum(last_pick * seg_weights, axis=1)
    continued = (ancestor[:, 0] < first_leaf).astype(jnp.float32)
    spanning = (ancestor[:, leaves - 1] < first_leaf).astype(jnp.float32)
    head_sum = seg_sums[:, 0, :] * continued[:, None]
    head_weight = seg_weights[:, 0] * continued
    gathered = (
        lax.all_gather(tail_sum[None], "scen", axis=0, tiled=True),
        lax.all_gather(tail_weight[None], "scen", axis=0, tiled=True),
        lax.all_gather(head_sum[None], "scen", axis=0, tiled=True),
        lax.all_gather(head_weight[None], "scen", axis=0, tiled=True),
        lax.all_gather(spanning[None], "scen", axis=0, tiled=True),
    )
    position = lax.axis_index("scen")
    group_ids = jnp.arange(gathered[0].shape[0], dtype=jnp.int32)
    blank = (jnp.zeros_like(tail_sum), jnp.zeros_like(tail_weight), jnp.ones_like(spanning))

    def forward_step(carry, item):
        group, part_sum, part_weight, part_flag = item
        joined = link_terms(carry, (part_sum, part_weight, part_flag))
        keep = group < position
        return (
            jax.tree.map(lambda new_val, old_val: jnp.where(keep, new_val, old_val), joined, carry),
            None,
        )

    def backward_step(carry, item):
        group, part_sum, part_weight, part_flag = item
        joined = link_terms(carry, (part_sum, part_weight, part_flag))
        keep = group > position
        return (
            jax.tree.map(lambda new_val, old_val: jnp.where(keep, new_val, old_val), joined, carry),
            None,
        )

    before, unused = lax.scan(
        forward_step, blank, (group_ids, gathered[0], gathered[1], gathered[4])
    )
    after, unused = lax.scan(
        backward_step, blank, (group_ids, gathered[2], gathered[3], gathered[4]), reverse=True
    )
    open_front = first_pick * continued[:, None]
    seg_total = (
        seg_sums
        + open_front[:, :, None] * before[0][:, None, :]
        + last_pick[:, :, None] * after[0][:, None, :]
    )
    weight_total = seg_weights + open_front * before[1][:, None] + last_pick * after[1][:, None]
    leaf_sums = jnp.einsum("tgl,tgn->ltn", member, seg_total, precision=highest)
    leaf_weights = jnp.einsum("tgl,tg->lt", member, weight_total, precision=highest)
    average = leaf_sums / leaf_weights[:, :, None]
    new_dual = dual + penalty * (state - average)
    return (state, average, new_dual)


def solution(mesh):
    return jax.shard_map(
        local,
        mesh=mesh,
        in_specs=(
            P("scen", None, "feeder"),
            P("scen", None, "feeder"),
            P("scen", None, "feeder"),
            P("scen", None),
            P("scen"),
            P("feeder", None),
            P("feeder"),
            P("feeder", None, None),
            P(None, "scen"),
        ),
        out_specs=(P("scen", None, "feeder"), P("scen", None, "feeder"), P("scen", None, "feeder")),
        check_vma=False,
    )
```

profile of v0, /device:TPU:32, one launch (start us, length us, event | category | flops | bytes accessed | tf_op | source)
XLA Modules:
  0.0 681.2 jit_solution(15530600553333728089)
XLA Ops:
  0.6 0.7 convert_bitcast_fusion
  1.4 0.6 broadcast_in_dim.11
  2.1 0.9 copy-done
  3.0 0.4 fusion.100
  3.9 68.3 %psum.56 = f32[16,24]{1,0:T(8,128)S(1)} all-reduce(f32[16,24]{1,0:T(8,128)S(1)} %convert_reduce_fusion), channel_id=1, replica_groups=mesh['feeder'=32,'scen'=16] {'feeder'}, use_global_device_ids=true, to_apply=%region_1.0 | all-reduce | flops 384 | bytes 3072 | tf_op jit(solution)/shard_map/psum | solution.py:38
  72.2 1.4 fusion.74
  73.6 63.7 %psum.57 = f32[16,24]{1,0:T(8,128)S(1)} all-reduce(f32[16,24]{1,0:T(8,128)S(1)} %get-tuple-element.314), channel_id=1, replica_groups=mesh['feeder'=32,'scen'=16] {'feeder'}, use_global_device_ids=true, to_apply=%region_3.4 | all-reduce | flops 384 | bytes 3072 | tf_op jit(solution)/shard_map/psum | solution.py:38
  137.4 0.9 fusion.93
  138.2 63.7 %psum.58 = f32[16,24]{1,0:T(8,128)S(1)} all-reduce(f32[16,24]{1,0:T(8,128)S(1)} %get-tuple-element.320), channel_id=1, replica_groups=mesh['feeder'=32,'scen'=16] {'feeder'}, use_global_device_ids=true, to_apply=%region_5.6 | all-reduce | flops 384 | bytes 3072 | tf_op jit(solution)/shard_map/psum | solution.py:38
  201.9 0.6 fusion.94
  202.5 63.7 %psum.59 = f32[16,24]{1,0:T(8,128)S(1)} all-reduce(f32[16,24]{1,0:T(8,128)S(1)} %get-tuple-element.322), channel_id=1, replica_groups=mesh['feeder'=32,'scen'=16] {'feeder'}, use_global_device_ids=true, to_apply=%region_7.8 | all-reduce | flops 384 | bytes 3072 | tf_op jit(solution)/shard_map/psum | solution.py:38
  266.2 0.6 fusion.95
  266.8 63.7 %psum.60 = f32[16,24]{1,0:T(8,128)S(1)} all-reduce(f32[16,24]{1,0:T(8,128)S(1)} %get-tuple-element.324), channel_id=1, replica_groups=mesh['feeder'=32,'scen'=16] {'feeder'}, use_global_device_ids=true, to_apply=%region_9.10 | all-reduce | flops 384 | bytes 3072 | tf_op jit(solution)/shard_map/psum | solution.py:38
  330.5 0.6 fusion.96
  331.1 63.7 %psum.61 = f32[16,24]{1,0:T(8,128)S(1)} all-reduce(f32[16,24]{1,0:T(8,128)S(1)} %get-tuple-element.326), channel_id=1, replica_groups=mesh['feeder'=32,'scen'=16] {'feeder'}, use_global_device_ids=true, to_apply=%region_11.12 | all-reduce | flops 384 | bytes 3072 | tf_op jit(solution)/shard_map/psum | solution.py:38
  394.8 1.4 fusion.97
  396.1 63.7 %psum.62 = f32[16,24]{1,0:T(8,128)S(1)} all-reduce(f32[16,24]{1,0:T(8,128)S(1)} %get-tuple-element.328), channel_id=1, replica_groups=mesh['feeder'=32,'scen'=16] {'feeder'}, use_global_device_ids=true, to_apply=%region_13.14 | all-reduce | flops 384 | bytes 3072 | tf_op jit(solution)/shard_map/psum | solution.py:38
  459.8 2.0 fusion.98
  461.8 63.7 %psum.63 = f32[16,24]{1,0:T(8,128)S(1)} all-reduce(f32[16,24]{1,0:T(8,128)S(1)} %get-tuple-element.330), channel_id=1, replica_groups=mesh['feeder'=32,'scen'=16] {'feeder'}, use_global_device_ids=true, to_apply=%region_15.16 | all-reduce | flops 384 | bytes 3072 | tf_op jit(solution)/shard_map/psum | solution.py:38
  525.5 0.6 copy-done.8
  526.2 1.4 broadcast_multiply_fusion
  527.5 0.7 copy-done.6
  528.3 1.0 fusion.48
  529.5 0.4 fusion.99
  529.9 37.7 %all-gather = f32[384,512]{1,0:T(8,128)S(1)} all-gather(f32[24,512]{1,0:T(8,128)S(1)} %bitcast.122), channel_id=2, replica_groups=mesh['feeder'=32,'scen'=16] {'scen'}, dimensions={0}, use_global_device_ids=true | all-gather | bytes 835584 | tf_op jit(solution)/shard_map/all_gather | solution.py:59
  568.0 1.3 dynamic-slice
  570.3 30.1 %all-reduce.3 = (f32[384]{0:T(512)S(1)}, f32[384]{0:T(512)S(1)}, f32[384]{0:T(512)S(1)}) all-reduce(f32[384]{0:T(512)S(1)} %fusion.86, f32[384]{0:T(512)S(1)} %fusion.84, f32[384]{0:T(512)S(1)} %dynamic-update-slice.1), channel_id=3, replica_groups=mesh['feeder'=32,'scen'=16] {'scen'}, use_global_device_ids=true, to_apply=%add | all-reduce | flops 1152 | bytes 9216
  600.6 23.5 %while.30 = (s32[]{:T(128)}, f32[24,512]{1,0:T(8,128)S(1)}, f32[24]{0:T(128)S(1)}, s32[16]{0:T(128)S(1)}, s32[]{:T(128)}, /*index=5*/f32[16,24,512]{2,1,0:T(8,12...) while((s32[]{:T(128)}, f32[24,512]{1,0:T(8,128)S(1)}, ...), condition=%wide.region_18.19_spmd.clone, body=%wide.region_17.18_spmd.clone.sunk | while | flops 49252 | bytes 148175 | solution.py:87
  600.6 0.7 dynamic_slice.91
  602.1 0.7 dynamic_slice.91
  603.5 0.7 dynamic_slice.91
  605.0 0.7 dynamic_slice.91
  606.5 0.7 dynamic_slice.91
  607.9 0.7 dynamic_slice.91
  609.4 0.7 dynamic_slice.91
  610.9 0.7 dynamic_slice.91
  612.3 0.7 dynamic_slice.91
  613.8 0.7 dynamic_slice.91
  615.3 0.7 dynamic_slice.91
  616.7 0.7 dynamic_slice.91
  618.2 0.7 dynamic_slice.91
  619.7 0.7 dynamic_slice.91
  621.1 0.7 dynamic_slice.91
  622.6 0.7 dynamic_slice.91
  624.2 30.1 %all_gather.18 = f32[16,24,512]{2,1,0:T(8,128)S(1)} all-gather(f32[1,24,512]{2,1,0:T(8,128)S(1)} %copy.24), channel_id=1, replica_groups=mesh['feeder'=32,'scen'=16] {'scen'}, dimensions={0}, use_global_device_ids=true | all-gather | bytes 835584 | tf_op jit(solution)/shard_map/all_gather | solution.py:61
  654.4 23.5 %while.31 = (s32[]{:T(128)}, f32[24,512]{1,0:T(8,128)S(1)}, f32[24]{0:T(128)S(1)}, s32[16]{0:T(128)S(1)}, s32[]{:T(128)}, /*index=5*/f32[16,24,512]{2,1,0:T(8,12...) while((s32[]{:T(128)}, f32[24,512]{1,0:T(8,128)S(1)}, ...), condition=%wide.region_20.21_spmd.clone, body=%wide.region_19.20_spmd.clone.sunk | while | flops 49253 | bytes 148195 | solution.py:90
  654.4 0.7 dynamic_slice.94
  655.9 0.7 dynamic_slice.94
  657.4 0.7 dynamic_slice.94
  658.9 0.7 dynamic_slice.94
  660.3 0.7 dynamic_slice.94
  661.8 0.7 dynamic_slice.94
  663.3 0.7 dynamic_slice.94
  664.7 0.7 dynamic_slice.94
  666.2 0.7 dynamic_slice.94
  667.7 0.7 dynamic_slice.94
  669.1 0.7 dynamic_slice.94
  670.6 0.7 dynamic_slice.94
  672.1 0.7 dynamic_slice.94
  673.5 0.7 dynamic_slice.94
  675.0 0.7 dynamic_slice.94
  676.5 0.7 dynamic_slice.94
  678.2 0.7 fusion.50
  679.5 1.7 subtract_add_fusion
  (125 shorter events, 6.0 us)
Async XLA Ops:
  0.6 1.4 copy-start.4
  2.0 1.0 copy-start
  3.0 0.7 copy-start.7
  3.0 69.2 %copy-start.2 = (f32[16,24,512]{2,1,0:T(8,128)S(1)}, f32[16,24,512]{2,1,0:T(8,128)}, u32[]{:S(2)}) copy-start(f32[16,24,512]{2,1,0:T(8,128)} %param.15) | copy-start | bytes 2359300
  3.8 68.4 %copy-start.5 = (f32[16,24]{1,0:T(8,128)S(1)}, f32[16,24]{1,0:T(8,128)}, u32[]{:S(2)}) copy-start(f32[16,24]{1,0:T(8,128)} %param.16) | copy-start | bytes 4612
  525.5 0.7 copy-start.8
  527.5 0.7 copy-start.6
  678.2 1.1 copy-start.1
  678.2 1.4 copy-start.3
where the time goes:
time: 682 us; the launch traced here: 681 us
  blocking collectives  612 us (90%)
  local copies, waits for them, and re-layouts  27 us (4%)
  loops' own time  22.6 us (3%)
  matrix products  10.1 us (1%)
  other arithmetic  7.87 us (1%)
    psum x8, blocking collectives, local(): head = lax.psum(jnp.sum(state, axis=2), 'feeder') / total_nodes  514 us
    all_gather x1, blocking collectives, local(): lax.all_gather(tail_sum[None], 'scen', axis=0, tiled=True)  37.7 us
    all_gather x1, blocking collectives, local(): lax.all_gather(head_sum[None], 'scen', axis=0, tiled=True)  30.1 us
    unnamed x1, blocking collectives  30.1 us
    dynamic_slice x32, local copies, waits for them, and re-layouts, local(): lax.scan(forward_step, blank, (group_ids, gathered[0], gathered[1], gathe...  21.2 us

commit v1 on v0

--- a/solution.py
+++ b/solution.py
@@ -35,7 +35,7 @@
     for sweep in range(PROX_ITERS):
         flat = state.reshape(rows, nodes).astype(jnp.bfloat16)
         image = jnp.dot(flat, q_eff, preferred_element_type=jnp.float32)
-        head = lax.psum(jnp.sum(state, axis=2), "feeder") / total_nodes
+        head = jnp.sum(lax.all_gather(jnp.sum(state, axis=2), "feeder"), axis=0) / total_nodes
         grad = image.reshape(leaves, sections, nodes) + diag_term * state + fixed_part
         grad = grad + coupling * (head - target)[:, :, None]
         state = jnp.clip(state - step_size * grad, -power_limit, power_limit)

time: 682 us -> 359 us (0.53)
  the two profiles are of different devices: /device:TPU:32 before, /device:TPU:4 now
where the time goes in v1:
time: 359 us; the launch traced here: 358 us
  blocking collectives  288 us (80%)
  local copies, waits for them, and re-layouts  27.7 us (8%)
  loops' own time  22.6 us (6%)
  matrix products  10.2 us (3%)
  other arithmetic  8.21 us (2%)
    all_gather x8, blocking collectives, local(): lax.all_gather(jnp.sum(state, axis=2), 'feeder')  191 us
    all_gather x1, blocking collectives, local(): lax.all_gather(tail_sum[None], 'scen', axis=0, tiled=True)  37.2 us
    all_gather x1, blocking collectives, local(): lax.all_gather(head_sum[None], 'scen', axis=0, tiled=True)  32.1 us
    unnamed x1, blocking collectives  27.5 us
    dynamic_slice x32, local copies, waits for them, and re-layouts, local(): lax.scan(forward_step, blank, (group_ids, gathered[0], gathered[1], gathe...  21.2 us
    another operation x1, loops' own time, local(): lax.scan(backward_step, blank, (group_ids, gathered[2], gathered[3], gath...  11.3 us
    another operation x1, loops' own time, local(): lax.scan(forward_step, blank, (group_ids, gathered[0], gathered[1], gathe...  11.3 us
    dot_general x8, matrix products, local(): image = jnp.dot(flat, q_eff, preferred_element_type=jnp.float32)  7.77 us

profile of v1, /device:TPU:4, one launch (start us, length us, event | category | flops | bytes accessed | tf_op | source)
XLA Modules:
  0.0 358.4 jit_solution(13315539829135253379)
XLA Ops:
  0.6 0.7 convert_bitcast_fusion
  1.4 0.6 broadcast_in_dim.11
  2.1 0.9 copy-done
  3.8 25.7 %all-gather = f32[512,24]{1,0:T(8,128)S(1)} all-gather(f32[16,24]{1,0:T(8,128)S(1)} %convert_reduce_fusion), channel_id=2, replica_groups=mesh['feeder'=32,'scen'=16] {'feeder'}, dimensions={0}, use_global_device_ids=true | all-gather | bytes 50688 | tf_op jit(solution)/shard_map/all_gather | solution.py:38
  29.6 0.7 copy-done.5
  30.3 1.4 fusion.74
  31.7 24.9 %all-gather.1 = f32[512,24]{1,0:T(8,128)S(1)} all-gather(f32[16,24]{1,0:T(8,128)S(1)} %get-tuple-element.314), channel_id=3, replica_groups=mesh['feeder'=32,'scen'=16] {'feeder'}, dimensions={0}, use_global_device_ids=true | all-gather | bytes 50688 | tf_op jit(solution)/shard_map/all_gather | solution.py:38
  56.7 0.9 fusion.93
  57.6 22.2 %all-gather.2 = f32[512,24]{1,0:T(8,128)S(1)} all-gather(f32[16,24]{1,0:T(8,128)S(1)} %get-tuple-element.320), channel_id=4, replica_groups=mesh['feeder'=32,'scen'=16] {'feeder'}, dimensions={0}, use_global_device_ids=true | all-gather | bytes 50688 | tf_op jit(solution)/shard_map/all_gather | solution.py:38
  79.8 0.6 fusion.94
  80.4 24.7 %all-gather.3 = f32[512,24]{1,0:T(8,128)S(1)} all-gather(f32[16,24]{1,0:T(8,128)S(1)} %get-tuple-element.322), channel_id=5, replica_groups=mesh['feeder'=32,'scen'=16] {'feeder'}, dimensions={0}, use_global_device_ids=true | all-gather | bytes 50688 | tf_op jit(solution)/shard_map/all_gather | solution.py:38
  105.1 0.6 fusion.95
  105.7 22.2 %all-gather.4 = f32[512,24]{1,0:T(8,128)S(1)} all-gather(f32[16,24]{1,0:T(8,128)S(1)} %get-tuple-element.324), channel_id=6, replica_groups=mesh['feeder'=32,'scen'=16] {'feeder'}, dimensions={0}, use_global_device_ids=true | all-gather | bytes 50688 | tf_op jit(solution)/shard_map/all_gather | solution.py:38
  127.9 0.6 fusion.96
  128.5 24.9 %all-gather.5 = f32[512,24]{1,0:T(8,128)S(1)} all-gather(f32[16,24]{1,0:T(8,128)S(1)} %get-tuple-element.326), channel_id=7, replica_groups=mesh['feeder'=32,'scen'=16] {'feeder'}, dimensions={0}, use_global_device_ids=true | all-gather | bytes 50688 | tf_op jit(solution)/shard_map/all_gather | solution.py:38
  153.4 1.4 fusion.97
  154.8 22.2 %all-gather.6 = f32[512,24]{1,0:T(8,128)S(1)} all-gather(f32[16,24]{1,0:T(8,128)S(1)} %get-tuple-element.328), channel_id=8, replica_groups=mesh['feeder'=32,'scen'=16] {'feeder'}, dimensions={0}, use_global_device_ids=true | all-gather | bytes 50688 | tf_op jit(solution)/shard_map/all_gather | solution.py:38
  177.0 1.9 fusion.98
  179.0 24.7 %all-gather.7 = f32[512,24]{1,0:T(8,128)S(1)} all-gather(f32[16,24]{1,0:T(8,128)S(1)} %get-tuple-element.330), channel_id=9, replica_groups=mesh['feeder'=32,'scen'=16] {'feeder'}, dimensions={0}, use_global_device_ids=true | all-gather | bytes 50688 | tf_op jit(solution)/shard_map/all_gather | solution.py:38
  203.7 0.6 copy-done.8
  204.3 1.4 broadcast_multiply_fusion
  205.8 0.7 copy-done.6
  206.5 1.0 fusion.48
  207.7 0.4 fusion.99
  208.1 37.2 %all-gather.8 = f32[384,512]{1,0:T(8,128)S(1)} all-gather(f32[24,512]{1,0:T(8,128)S(1)} %bitcast.138), channel_id=10, replica_groups=mesh['feeder'=32,'scen'=16] {'scen'}, dimensions={0}, use_global_device_ids=true | all-gather | bytes 835584 | tf_op jit(solution)/shard_map/all_gather | solution.py:59
  245.7 1.3 dynamic-slice
  248.0 27.5 %all-reduce.3 = (f32[384]{0:T(512)S(1)}, f32[384]{0:T(512)S(1)}, f32[384]{0:T(512)S(1)}) all-reduce(f32[384]{0:T(512)S(1)} %fusion.86, f32[384]{0:T(512)S(1)} %fusion.84, f32[384]{0:T(512)S(1)} %dynamic-update-slice.1), channel_id=11, replica_groups=mesh['feeder'=32,'scen'=16] {'scen'}, use_global_device_ids=true, to_apply=%add | all-reduce | flops 1152 | bytes 9216
  275.7 23.5 %while.30 = (s32[]{:T(128)}, f32[24,512]{1,0:T(8,128)S(1)}, f32[24]{0:T(128)S(1)}, s32[16]{0:T(128)S(1)}, s32[]{:T(128)}, /*index=5*/f32[16,24,512]{2,1,0:T(8,12...) while((s32[]{:T(128)}, f32[24,512]{1,0:T(8,128)S(1)}, ...), condition=%wide.region_18.19_spmd.clone, body=%wide.region_17.18_spmd.clone.sunk | while | flops 49252 | bytes 148175 | solution.py:87
  275.8 0.7 dynamic_slice.91
  277.2 0.7 dynamic_slice.91
  278.7 0.7 dynamic_slice.91
  280.2 0.7 dynamic_slice.91
  281.6 0.7 dynamic_slice.91
  283.1 0.7 dynamic_slice.91
  284.6 0.7 dynamic_slice.91
  286.0 0.7 dynamic_slice.91
  287.5 0.7 dynamic_slice.91
  289.0 0.7 dynamic_slice.91
  290.4 0.7 dynamic_slice.91
  291.9 0.7 dynamic_slice.91
  293.4 0.7 dynamic_slice.91
  294.8 0.7 dynamic_slice.91
  296.3 0.7 dynamic_slice.91
  297.8 0.7 dynamic_slice.91
  299.3 32.1 %all_gather.82 = f32[16,24,512]{2,1,0:T(8,128)S(1)} all-gather(f32[1,24,512]{2,1,0:T(8,128)S(1)} %copy.69), channel_id=1, replica_groups=mesh['feeder'=32,'scen'=16] {'scen'}, dimensions={0}, use_global_device_ids=true | all-gather | bytes 835584 | tf_op jit(solution)/shard_map/all_gather | solution.py:61
  331.6 23.5 %while.31 = (s32[]{:T(128)}, f32[24,512]{1,0:T(8,128)S(1)}, f32[24]{0:T(128)S(1)}, s32[16]{0:T(128)S(1)}, s32[]{:T(128)}, /*index=5*/f32[16,24,512]{2,1,0:T(8,12...) while((s32[]{:T(128)}, f32[24,512]{1,0:T(8,128)S(1)}, ...), condition=%wide.region_20.21_spmd.clone, body=%wide.region_19.20_spmd.clone.sunk | while | flops 49253 | bytes 148195 | solution.py:90
  331.6 0.7 dynamic_slice.94
  333.1 0.7 dynamic_slice.94
  334.5 0.7 dynamic_slice.94
  336.0 0.7 dynamic_slice.94
  337.5 0.7 dynamic_slice.94
  338.9 0.7 dynamic_slice.94
  340.4 0.7 dynamic_slice.94
  341.9 0.7 dynamic_slice.94
  343.3 0.7 dynamic_slice.94
  344.8 0.7 dynamic_slice.94
  346.3 0.7 dynamic_slice.94
  347.7 0.7 dynamic_slice.94
  349.2 0.7 dynamic_slice.94
  350.7 0.7 dynamic_slice.94
  352.1 0.7 dynamic_slice.94
  353.6 0.7 dynamic_slice.94
  355.3 0.7 fusion.50
  356.7 1.7 subtract_add_fusion
  (133 shorter events, 6.7 us)
Async XLA Ops:
  0.6 1.4 copy-start.4
  2.0 1.0 copy-start
  3.0 0.7 copy-start.7
  3.4 26.9 %copy-start.2 = (f32[16,24,512]{2,1,0:T(8,128)S(1)}, f32[16,24,512]{2,1,0:T(8,128)}, u32[]{:S(2)}) copy-start(f32[16,24,512]{2,1,0:T(8,128)} %param.15) | copy-start | bytes 2359300
  29.6 0.7 copy-start.5
  203.7 0.7 copy-start.8
  205.7 0.7 copy-start.6
  355.3 1.1 copy-start.1
  355.3 1.4 copy-start.3
